TPU v7x, 32 devices: a whole 2x2x4 slice. The times are simulated.
32 devices in a mesh: group: 2 (over y), slab: 4 (over z), subj: 2 (over x), yslab: 2 (over core).
Axes of the slice: x: 2, y: 2, z: 4, core: 2. Of those that a mesh axis runs over, the one named last changes fastest.
Arguments:
- subjects: bfloat16 [4, 64, 16, 256], P(('group', 'subj'), 'slab', 'yslab'), parts along dimension 0, may hold values from -6 to 6
- offsets: int32 [4, 3, 64, 16, 256], P(('group', 'subj'), None, 'slab', 'yslab'), parts along dimension 0, may hold values from -2 to 1
- template: float32 [128, 16, 256], P(('group', 'slab'), 'yslab'), parts along dimension 0, may hold values from -6 to 6
- control: float32 [4, 3, 19, 7, 128], P(('group', 'subj')), parts along dimension 0, may hold values from -8 to 8
Outputs:
- template_out: float32 [128, 16, 256], P(('group', 'slab'), 'yslab'), parts along dimension 0
- control_out: float32 [4, 3, 19, 7, 128], P(('group', 'subj')), parts along dimension 0
There are 2 independent parts, one for each index of `group`. A program takes and returns all parts, laid end to end along the dimension named above; each array names one. Nothing has to cross between parts.
All inputs are finite; a program needn't handle non-finite values.
Results may differ from a plain program's by a relative error of at most 0.00065.
Values may be sent and summed in bfloat16 or wider, within the bound.
A program may use at most 64 MiB of HBM per device.

v0:
```python
import jax
import jax.numpy as jnp
from jax import lax
from jax.sharding import PartitionSpec as P

KNOT = 4
KNOT_X = 2
HALO = 2
ITERS = 2


step_length = 0.5
tiny_term = 1e-06


def extended_2(value, sides, width):
    for axis, dim in sides:
        peers, length = (lax.axis_size(axis), value.shape[dim])
        up = [(i, (i + 1) % peers) for i in range(peers - 1)]
        down = [(j, i) for i, j in up]
        last = lax.slice_in_dim(value, length - width, length, axis=dim)
        initial = lax.slice_in_dim(value, 0, width, axis=dim)
        before = lax.ppermute(last, axis, up)
        after = lax.ppermute(initial, axis, down)
        value = jnp.concatenate([before, value, after], axis=dim)
    return value


def shifted(block, axis, distance):
    devices = range(lax.axis_size(axis))
    route = [(i - distance, i) for i in devices if i - distance in devices]
    return lax.ppermute(block, axis, route)


def from_root(value, axis, source):
    kept = jnp.where(lax.axis_index(axis) == source, value, 0).astype(value.dtype)
    return lax.psum(kept, axis)


def basis(positions, columns, spacing, wrap):
    cell = positions // spacing
    frac = (positions - cell * spacing).astype(jnp.float32) / spacing
    weights = [
        (1.0 - frac) ** 3 / 6.0,
        (3.0 * frac**3 - 6.0 * frac**2 + 4.0) / 6.0,
        (-3.0 * frac**3 + 3.0 * frac**2 + 3.0 * frac + 1.0) / 6.0,
        frac**3 / 6.0,
    ]
    index = jnp.arange(columns, dtype=jnp.int32)
    matrix = jnp.zeros((positions.shape[0], columns), jnp.float32)
    for offset in range(4):
        target = cell + offset
        if wrap:
            target = target % columns
        matrix = matrix + jnp.where(
            index[None, :] == target[:, None], weights[offset][:, None], 0.0
        )
    return matrix


def forward_field(coeffs, basis_z, basis_y, basis_x):
    high = lax.Precision.HIGHEST
    first = jnp.einsum("cabg,za->czbg", coeffs, basis_z, precision=high)
    second = jnp.einsum("czbg,yb->czyg", first, basis_y, precision=high)
    return jnp.einsum("czyg,xg->czyx", second, basis_x, precision=high)


def adjoint_field(gradient, basis_z, basis_y, basis_x):
    high = lax.Precision.HIGHEST
    first = jnp.einsum("czyx,xg->czyg", gradient, basis_x, precision=high)
    second = jnp.einsum("czyg,yb->czbg", first, basis_y, precision=high)
    return jnp.einsum("czbg,za->cabg", second, basis_z, precision=high)


def choose(shift_of, table, lead):
    result = table[-HALO + lead]
    for value in range(-HALO + 1, HALO):
        result = jnp.where(shift_of == value, table[value + lead], result)
    return result


def trilinear_local(volume, shifts, fraction, depth, height, width):
    frac_z, frac_y, frac_x = (fraction[0], fraction[1], fraction[2])
    shift_z, shift_y, shift_x = (shifts[0], shifts[1], shifts[2])
    along_y_of = {}
    diff_y_of = {}
    diff_xy_of = {}
    for move_z in range(-HALO, HALO + 1):
        along_x_of = {}
        diff_x_of = {}
        for move_y in range(-HALO, HALO + 1):
            plane = volume[
                move_z + HALO : move_z + HALO + depth, move_y + HALO : move_y + HALO + height, :
            ].astype(jnp.float32)
            columns = {}
            for move_x in range(-HALO, HALO + 1):
                columns[move_x] = plane[:, :, move_x + HALO : move_x + HALO + width]
            low = choose(shift_x, columns, 0)
            high = choose(shift_x, columns, 1)
            along_x_of[move_y] = low * (1.0 - frac_x) + high * frac_x
            diff_x_of[move_y] = high - low
        along_low = choose(shift_y, along_x_of, 0)
        along_high = choose(shift_y, along_x_of, 1)
        diff_low = choose(shift_y, diff_x_of, 0)
        diff_high = choose(shift_y, diff_x_of, 1)
        along_y_of[move_z] = along_low * (1.0 - frac_y) + along_high * frac_y
        diff_y_of[move_z] = along_high - along_low
        diff_xy_of[move_z] = diff_low * (1.0 - frac_y) + diff_high * frac_y
    along_y = [choose(shift_z, along_y_of, 0), choose(shift_z, along_y_of, 1)]
    diff_y = [choose(shift_z, diff_y_of, 0), choose(shift_z, diff_y_of, 1)]
    diff_xy = [choose(shift_z, diff_xy_of, 0), choose(shift_z, diff_xy_of, 1)]
    warped = along_y[0] * (1.0 - frac_z) + along_y[1] * frac_z
    slope_z = along_y[1] - along_y[0]
    slope_y = diff_y[0] * (1.0 - frac_z) + diff_y[1] * frac_z
    slope_x = diff_xy[0] * (1.0 - frac_z) + diff_xy[1] * frac_z
    return (warped, jnp.stack([slope_z, slope_y, slope_x]))


def shards(subjects, offsets, template, control):
    local_subjects = subjects.shape[0]
    depth, height, width = (subjects.shape[1], subjects.shape[2], subjects.shape[3])
    rows_slab = depth // KNOT
    cohort = local_subjects * lax.axis_size("subj")
    extended = extended_2(subjects, (("slab", 1), ("yslab", 2)), HALO)
    extended = jnp.pad(extended, ((0, 0), (0, 0), (0, 0), (HALO, HALO)))
    basis_z = basis(jnp.arange(depth, dtype=jnp.int32), rows_slab + 3, KNOT, False)
    y_start = lax.axis_index("yslab") * height
    basis_y = basis(y_start + jnp.arange(height, dtype=jnp.int32), control.shape[3], KNOT, False)
    basis_x = basis(jnp.arange(width, dtype=jnp.int32), control.shape[4], KNOT_X, True)
    first_row = lax.axis_index("slab") * rows_slab
    current = template
    coeffs_all = control
    for iteration in range(ITERS):
        band_coeffs = lax.dynamic_slice_in_dim(coeffs_all[0], first_row, rows_slab + 3, 1)
        displace = forward_field(band_coeffs, basis_z, basis_y, basis_x)
        tanh_u = jnp.tanh(displace)
        fraction = 0.5 + 0.5 * tanh_u
        warped, slopes = trilinear_local(extended[0], offsets[0], fraction, depth, height, width)
        resid = warped - current
        grad_u = resid[None] * slopes * (1.0 - tanh_u * tanh_u)
        band_list = [adjoint_field(grad_u, basis_z, basis_y, basis_x)]
        band_grid = jnp.stack(band_list)
        current = lax.psum(warped, "subj") / cohort
        band_grid = lax.psum(band_grid.astype(jnp.bfloat16), "yslab").astype(jnp.float32)
        head_rows = band_grid[:, :, :rows_slab]
        tail_part = band_grid[:, :, rows_slab:]
        carried = shifted(tail_part, "slab", 1)
        head_rows = head_rows.at[:, :, :3].add(carried)
        owned = lax.all_gather(head_rows.astype(jnp.bfloat16), "slab", axis=2, tiled=True).astype(
            head_rows.dtype
        )
        last_part = from_root(tail_part, "slab", lax.axis_size("slab") - 1)
        grid = jnp.concatenate([owned, last_part], axis=2)
        lengths = jnp.sqrt(jnp.sum(grid * grid, axis=1))
        peak = jnp.max(lengths, axis=(1, 2, 3))
        coeffs_all = coeffs_all - step_length * grid / (peak[:, None, None, None, None] + tiny_term)
    return (current, coeffs_all)


def solution(mesh):
    in_specs = (
        P(("group", "subj"), "slab", "yslab", None),
        P(("group", "subj"), None, "slab", "yslab", None),
        P(("group", "slab"), "yslab", None),
        P(("group", "subj"), None, None, None, None),
    )
    out_specs = (P(("group", "slab"), "yslab", None), P(("group", "subj"), None, None, None, None))
    return jax.shard_map(shards, mesh=mesh, in_specs=in_specs, out_specs=out_specs, check_vma=False)
```

profile of v0, /device:TPU:0, one launch (start us, length us, event | category | flops | bytes accessed | tf_op | source)
XLA Modules:
  0.0 160.3 jit_solution(13082636263804256856)
XLA Ops:
  7.9 1.3 collective-permute-start.1
  9.2 5.6 %collective-permute-start = (bf16[1,2,8,256]{3,2,1,0:T(8,128)(2,1)S(1)}, bf16[1,2,8,256]{3,2,1,0:T(8,128)(2,1)S(1)}, u32[]{:S(2)}, u32[]{:S(2)}) collective-permute-start(bf16[1,2,8,256]{3,2,1,0:T(8,128)(2,1)S(1)} %get-tuple-element.162), channel_id=1, source_target_pairs={{0,4},{4,8},{8,12},{1,5},{5,9},{9,13},{2,6},{6,10},{10,14},{3,7},{... | collective-permute-start | bytes 24584 | tf_op jit(solution)/shard_map/ppermute | solution.py:23
  15.2 0.9 constant_dynamic-slice_fusion
  17.6 1.5 collective-permute-start.2
  19.0 1.3 collective-permute-start.3
  20.4 1.5 multiply_add_fusion.1
  25.5 3.3 %fusion.335 = (f32[16,8,256]{2,1,0:T(8,128)S(1)}, f32[16,8,256]{2,1,0:T(8,128)}, f32[16,8,256]{2,1,0:T(8,128)S(1)}, f32[16,8,256]{2,1,0:T(8,128)S(1)}, f32[16,8,...) fusion(f32[16,8,256]{2,1,0:T(8,128)S(1)} %copy-done.64, ...), kind=kLoop, calls=%fused_computation.598 | loop fusion | flops 8093696 | bytes 21266432 | tf_op jit(solution)/shard_map/sub | solution.py:139
  30.5 2.9 %add_bitcast_fusion.2 = (f32[1,16,8,256]{3,2,1,0:T(8,128)S(1)}, f32[16,8,256]{2,1,0:T(8,128)}, f32[16,8,256]{2,1,0:T(8,128)}, f32[16,8,256]{2,1,0:T(8,128)}, f32...) fusion(pred[1,1,16,8,256]{4,3,2,1,0:T(8,128)(4,1)S(1)} %get-tup, ...), kind=kLoop, calls=%fused_computation.248 | loop fusion | flops 2654208 | bytes 8454144 | tf_op jit(solution)/shard_map/stack | solution.py:116
  34.1 0.8 fusion.4
  35.9 4.2 %psum.42 = bf16[1,3,7,7,128]{4,2,3,1,0:T(8,128)(2,1)S(1)} all-reduce(bf16[1,3,7,7,128]{4,2,3,1,0:T(8,128)(2,1)S(1)} %fusion), channel_id=1, replica_groups=mesh['group'=2,'slab'=4,'subj'=2,'yslab'=2] {'yslab'}, use_global_device_ids=true, to_apply=%region_0.1 | all-reduce | flops 18816 | bytes 75264 | tf_op jit(solution)/shard_map/psum | solution.py:144
  40.8 3.8 %collective-permute-start.4 = (f32[1,3,3,7,128]{4,2,3,1,0:T(4,128)S(1)}, f32[1,3,3,7,128]{4,2,3,1,0:T(4,128)S(1)}, u32[]{:S(2)}, u32[]{:S(2)}) collective-permute-start(f32[1,3,3,7,128]{4,2,3,1,0:T(4,128)S(1)} %slice.1053), channel_id=1, source_target_pairs={{0,4},{4,8},{8,12},{1,5},{5,9},{9,13},{2,6},{6,10},{10,14},{3,7},{... | collective-permute-start | bytes 96776 | tf_op jit(solution)/shard_map/ppermute | solution.py:32
  44.6 17.6 %psum.43 = f32[1,3,3,7,128]{4,2,3,1,0:T(4,128)S(1)} all-reduce(f32[1,3,3,7,128]{4,2,3,1,0:T(4,128)S(1)} %broadcast_select_fusion.1), channel_id=1, replica_groups=mesh['group'=2,'slab'=4,'subj'=2,'yslab'=2] {'slab'}, use_global_device_ids=true, to_apply=%region_1.2 | all-reduce | flops 8064 | bytes 64512 | tf_op jit(solution)/shard_map/psum | solution.py:37
  63.2 13.4 %all_gather.6 = bf16[1,3,16,7,128]{4,3,1,0,2:T(8,128)(2,1)S(1)} all-gather(bf16[1,3,4,7,128]{4,3,1,0,2:T(8,128)(2,1)S(1)} %copy.8), channel_id=1, replica_groups=mesh['group'=2,'slab'=4,'subj'=2,'yslab'=2] {'slab'}, dimensions={2}, use_global_device_ids=true | all-gather | bytes 107520 | tf_op jit(solution)/shard_map/all_gather | solution.py:149
  78.1 1.1 copy_subtract_fusion
  80.2 1.5 multiply_add_fusion
  81.9 3.0 %subtract_bitcast_fusion = (f32[1,16,8,256]{3,2,1,0:T(8,128)}, f32[16,8,256]{2,1,0:T(8,128)S(1)}, f32[16,8,256]{2,1,0:T(8,128)S(1)}, f32[16,8,256]{2,1,0:T(8,128...) fusion(pred[1,1,16,8,256]{4,3,2,1,0:T(8,128)(4,1)S(1)} %get-tup, ...), kind=kLoop, calls=%fused_computation.191 | loop fusion | flops 4227072 | bytes 8716288 | tf_op jit(solution)/shard_map/stack | solution.py:116
  87.0 20.5 %all-reduce.4.cloned.1.call-done = (f32[16,8,256]{2,1,0:T(8,128)}, f32[16,8,256]{2,1,0:T(8,128)}) async-done(((f32[16,8,256]{2,1,0:T(8,128)}, f32[16,8,256]{2,1,0:T(8,128)}), (f32[16,8,256]{2,1,0:T(8,128)}, f32[16,8,256]{2,1,0:T(8,128)})) %all-reduce.4.cloned.1.call-update) | async-done | bytes 262160 | tf_op jit(solution)/shard_map/psum | solution.py:143
  107.5 0.9 multiply_subtract_fusion
  109.1 0.8 fusion.11
  111.0 3.5 %psum.46 = bf16[1,3,7,7,128]{4,2,3,1,0:T(8,128)(2,1)S(1)} all-reduce(bf16[1,3,7,7,128]{4,2,3,1,0:T(8,128)(2,1)S(1)} %fusion.1), channel_id=1, replica_groups=mesh['group'=2,'slab'=4,'subj'=2,'yslab'=2] {'yslab'}, use_global_device_ids=true, to_apply=%region_6.7 | all-reduce | flops 18816 | bytes 75264 | tf_op jit(solution)/shard_map/psum | solution.py:144
  116.1 3.4 %collective-permute-start.5 = (f32[1,3,3,7,128]{4,2,3,1,0:T(4,128)S(1)}, f32[1,3,3,7,128]{4,2,3,1,0:T(4,128)S(1)}, u32[]{:S(2)}, u32[]{:S(2)}) collective-permute-start(f32[1,3,3,7,128]{4,2,3,1,0:T(4,128)S(1)} %slice.1059), channel_id=1, source_target_pairs={{0,4},{4,8},{8,12},{1,5},{5,9},{9,13},{2,6},{6,10},{10,14},{3,7},{... | collective-permute-start | bytes 96776 | tf_op jit(solution)/shard_map/ppermute | solution.py:32
  119.5 17.6 %psum.47 = f32[1,3,3,7,128]{4,2,3,1,0:T(4,128)S(1)} all-reduce(f32[1,3,3,7,128]{4,2,3,1,0:T(4,128)S(1)} %broadcast_select_fusion), channel_id=1, replica_groups=mesh['group'=2,'slab'=4,'subj'=2,'yslab'=2] {'slab'}, use_global_device_ids=true, to_apply=%region_7.8 | all-reduce | flops 8064 | bytes 64512 | tf_op jit(solution)/shard_map/psum | solution.py:37
  138.0 13.2 %all_gather.7 = bf16[1,3,16,7,128]{4,3,1,0,2:T(8,128)(2,1)S(1)} all-gather(bf16[1,3,4,7,128]{4,3,1,0,2:T(8,128)(2,1)S(1)} %copy.12), channel_id=1, replica_groups=mesh['group'=2,'slab'=4,'subj'=2,'yslab'=2] {'slab'}, dimensions={2}, use_global_device_ids=true | all-gather | bytes 107520 | tf_op jit(solution)/shard_map/all_gather | solution.py:149
  152.6 0.9 copy.15
  (352 shorter events, 18.6 us)
Async XLA Ops:
  7.2 100.3 %all-reduce.4.cloned.1.call-start = ((), (), s32[]{:S(2)}) async-start(), calls=%async_computation | async-start | bytes 524288 | tf_op jit(solution)/shard_map/psum | solution.py:143
  7.9 9.6 %collective-permute-start.1 = (bf16[1,2,8,256]{3,2,1,0:T(8,128)(2,1)S(1)}, bf16[1,2,8,256]{3,2,1,0:T(8,128)(2,1)S(1)}, u32[]{:S(2)}, u32[]{:S(2)}) collective-permute-start(bf16[1,2,8,256]{3,2,1,0:T(8,128)(2,1)S(1)} %get-tuple-element.161), channel_id=1, source_target_pairs={{4,0},{8,4},{12,8},{5,1},{9,5},{13,9},{6,2},{10,6},{14,10},{7,3},{... | collective-permute-start | bytes 24584 | tf_op jit(solution)/shard_map/ppermute | solution.py:24
  9.2 7.9 %collective-permute-start = (bf16[1,2,8,256]{3,2,1,0:T(8,128)(2,1)S(1)}, bf16[1,2,8,256]{3,2,1,0:T(8,128)(2,1)S(1)}, u32[]{:S(2)}, u32[]{:S(2)}) collective-permute-start(bf16[1,2,8,256]{3,2,1,0:T(8,128)(2,1)S(1)} %get-tuple-element.162), channel_id=1, source_target_pairs={{0,4},{4,8},{8,12},{1,5},{5,9},{9,13},{2,6},{6,10},{10,14},{3,7},{... | collective-permute-start | bytes 24584 | tf_op jit(solution)/shard_map/ppermute | solution.py:23
  15.1 18.2 %copy-start.66 = (f32[256]{0:T(256)}, f32[256]{0:T(256)S(1)}, u32[]{:S(2)}) copy-start(f32[256]{0:T(256)S(1)} %get-tuple-element.189) | copy-start | bytes 3076
  15.2 5.2 %copy-start.69 = (s32[256]{0:T(256)}, s32[256]{0:T(256)S(1)}, u32[]{:S(2)}) copy-start(s32[256]{0:T(256)S(1)} %get-tuple-element.186) | copy-start | bytes 3076
  15.2 5.2 %copy-start.73 = (s32[256]{0:T(256)}, s32[256]{0:T(256)S(1)}, u32[]{:S(2)}) copy-start(s32[256]{0:T(256)S(1)} %get-tuple-element.187) | copy-start | bytes 3076
  17.1 3.3 %copy-start.77 = (s32[256]{0:T(256)}, s32[256]{0:T(256)S(1)}, u32[]{:S(2)}) copy-start(s32[256]{0:T(256)S(1)} %get-tuple-element.184) | copy-start | bytes 3076
  17.1 3.3 %copy-start.81 = (s32[256]{0:T(256)}, s32[256]{0:T(256)S(1)}, u32[]{:S(2)}) copy-start(s32[256]{0:T(256)S(1)} %get-tuple-element.185) | copy-start | bytes 3076
  17.6 4.3 %collective-permute-start.2 = (bf16[1,20,2,256]{3,2,1,0:T(2,128)(2,1)S(1)}, bf16[1,20,2,256]{3,2,1,0:T(2,128)(2,1)S(1)}, u32[]{:S(2)}, u32[]{:S(2)}) collective-permute-start(bf16[1,20,2,256]{3,2,1,0:T(2,128)(2,1)S(1)} %get-tuple-element.159), channel_id=1, source_target_pairs={{0,1},{2,3},{4,5},{6,7},{8,9},{10,11},{12,13},{14,15},{16,17},{18,... | collective-permute-start | bytes 61448 | tf_op jit(solution)/shard_map/ppermute | solution.py:23
  19.0 3.1 %collective-permute-start.3 = (bf16[1,20,2,256]{3,2,1,0:T(2,128)(2,1)S(1)}, bf16[1,20,2,256]{3,2,1,0:T(2,128)(2,1)S(1)}, u32[]{:S(2)}, u32[]{:S(2)}) collective-permute-start(bf16[1,20,2,256]{3,2,1,0:T(2,128)(2,1)S(1)} %get-tuple-element.160), channel_id=1, source_target_pairs={{1,0},{3,2},{5,4},{7,6},{9,8},{11,10},{13,12},{15,14},{17,16},{19,... | collective-permute-start | bytes 61448 | tf_op jit(solution)/shard_map/ppermute | solution.py:24
  40.8 21.4 %collective-permute-start.4 = (f32[1,3,3,7,128]{4,2,3,1,0:T(4,128)S(1)}, f32[1,3,3,7,128]{4,2,3,1,0:T(4,128)S(1)}, u32[]{:S(2)}, u32[]{:S(2)}) collective-permute-start(f32[1,3,3,7,128]{4,2,3,1,0:T(4,128)S(1)} %slice.1053), channel_id=1, source_target_pairs={{0,4},{4,8},{8,12},{1,5},{5,9},{9,13},{2,6},{6,10},{10,14},{3,7},{... | collective-permute-start | bytes 96776 | tf_op jit(solution)/shard_map/ppermute | solution.py:32
  78.0 3.7 %copy-start.30 = (f32[16,8,256]{2,1,0:T(8,128)S(1)}, f32[16,8,256]{2,1,0:T(8,128)}, u32[]{:S(2)}) copy-start(f32[16,8,256]{2,1,0:T(8,128)} %copy-done.29) | copy-start | bytes 393220
  78.0 3.7 %copy-start.32 = (f32[16,8,256]{2,1,0:T(8,128)S(1)}, f32[16,8,256]{2,1,0:T(8,128)}, u32[]{:S(2)}) copy-start(f32[16,8,256]{2,1,0:T(8,128)} %copy-done.31) | copy-start | bytes 393220
  78.1 3.7 %copy-start.34 = (f32[16,8,256]{2,1,0:T(8,128)S(1)}, f32[16,8,256]{2,1,0:T(8,128)}, u32[]{:S(2)}) copy-start(f32[16,8,256]{2,1,0:T(8,128)} %copy-done.33) | copy-start | bytes 393220
  78.1 3.7 %copy-start.36 = (f32[16,8,256]{2,1,0:T(8,128)S(1)}, f32[16,8,256]{2,1,0:T(8,128)}, u32[]{:S(2)}) copy-start(f32[16,8,256]{2,1,0:T(8,128)} %copy-done.35) | copy-start | bytes 393220
  78.1 3.7 %copy-start.38 = (f32[16,8,256]{2,1,0:T(8,128)S(1)}, f32[16,8,256]{2,1,0:T(8,128)}, u32[]{:S(2)}) copy-start(f32[16,8,256]{2,1,0:T(8,128)} %copy-done.37) | copy-start | bytes 393220
  86.8 20.7 %copy-start = (f32[16,8,256]{2,1,0:T(8,128)S(1)}, f32[16,8,256]{2,1,0:T(8,128)}, u32[]{:S(2)}) copy-start(f32[16,8,256]{2,1,0:T(8,128)} %get-tuple-element.116) | copy-start | bytes 393220
  86.8 21.6 %copy-start.62 = (f32[1,16,8,256]{3,2,1,0:T(8,128)S(1)}, f32[1,16,8,256]{3,2,1,0:T(8,128)}, u32[]{:S(2)}) copy-start(f32[1,16,8,256]{3,2,1,0:T(8,128)} %get-tuple-element.32) | copy-start | bytes 393220
  86.8 21.6 %copy-start.72 = (s32[256]{0:T(256)S(1)}, s32[256]{0:T(256)}, u32[]{:S(2)}) copy-start(s32[256]{0:T(256)} %copy-done.69) | copy-start | bytes 3076
  86.8 21.7 %copy-start.76 = (s32[256]{0:T(256)S(1)}, s32[256]{0:T(256)}, u32[]{:S(2)}) copy-start(s32[256]{0:T(256)} %copy-done.73) | copy-start | bytes 3076
  86.8 21.7 %copy-start.80 = (s32[256]{0:T(256)S(1)}, s32[256]{0:T(256)}, u32[]{:S(2)}) copy-start(s32[256]{0:T(256)} %copy-done.77) | copy-start | bytes 3076
  86.8 21.7 %copy-start.84 = (s32[256]{0:T(256)S(1)}, s32[256]{0:T(256)}, u32[]{:S(2)}) copy-start(s32[256]{0:T(256)} %copy-done.81) | copy-start | bytes 3076
  87.0 21.5 %copy-start.58 = (f32[3,16,8,256]{3,2,1,0:T(8,128)S(1)}, f32[3,16,8,256]{3,2,1,0:T(8,128)}, u32[]{:S(2)}) copy-start(f32[3,16,8,256]{3,2,1,0:T(8,128)} %get-tuple-element.167) | copy-start | bytes 1179652
  116.1 21.0 %collective-permute-start.5 = (f32[1,3,3,7,128]{4,2,3,1,0:T(4,128)S(1)}, f32[1,3,3,7,128]{4,2,3,1,0:T(4,128)S(1)}, u32[]{:S(2)}, u32[]{:S(2)}) collective-permute-start(f32[1,3,3,7,128]{4,2,3,1,0:T(4,128)S(1)} %slice.1059), channel_id=1, source_target_pairs={{0,4},{4,8},{8,12},{1,5},{5,9},{9,13},{2,6},{6,10},{10,14},{3,7},{... | collective-permute-start | bytes 96776 | tf_op jit(solution)/shard_map/ppermute | solution.py:32
  (125 other events, 157.0 us)
Sparse Core Ops, SparseCore 0:
  85.9 21.5 all-reduce.3
where the time goes:
time: 161 us; the launch traced here: 160 us
  blocking collectives  69.6 us (43%)
  waiting for transfers between devices  20.7 us (13%)
  between operations  17.3 us (11%)
  starting transfers between devices  16.8 us (10%)
  other arithmetic  16.6 us (10%)
  local copies, waits for them, and re-layouts  11.8 us (7%)
  matrix products  7.5 us (5%)
    psum x2, blocking collectives, from_root(): return lax.psum(kept, axis)  35.2 us
    all_gather x2, blocking collectives, shards(): lax.all_gather(head_rows.astype(jnp.bfloat16), 'slab', axis=2, tiled=True)  26.7 us
    psum x1, waiting for transfers between devices, shards(): current = lax.psum(warped, 'subj') / cohort  20.5 us
    unnamed x283, local copies, waits for them, and re-layouts  8.37 us
    psum x2, blocking collectives, shards(): lax.psum(band_grid.astype(jnp.bfloat16), 'yslab').astype(jnp.float32)  7.77 us
    ppermute x2, starting transfers between devices, shifted(): return lax.ppermute(block, axis, route)  7.15 us
    ppermute x2, starting transfers between devices, extended_2(): before = lax.ppermute(last, axis, up)  7.04 us
    another operation x6, other arithmetic, trilinear_local(): return (warped, jnp.stack([slope_z, slope_y, slope_x]))  6.89 us
  transfers between devices with their start and end apart: 7, of which 2 were waited for; matrix products, arithmetic and copies ran while one was open for 2% of the time, Pallas kernels for 0%

commit v1 on v0

v1 whole, which is shorter than its diff:
```python
import functools

import jax
import jax.numpy as jnp
from jax import lax
from jax.experimental import pallas as pl
from jax.experimental.pallas import tpu as pltpu
from jax.sharding import PartitionSpec as P

KNOT = 4
KNOT_X = 2
HALO = 2
ITERS = 2
SPAN = 2 * HALO + 1
LANES = 128
SUB = 8

step_length = 0.5
tiny_term = 1e-06

MESH = pl.DeviceIdType.MESH


def spline(step, spacing):
    s = step / spacing
    return (
        (1.0 - s) ** 3 / 6.0,
        (3.0 * s**3 - 6.0 * s**2 + 4.0) / 6.0,
        (-3.0 * s**3 + 3.0 * s**2 + 3.0 * s + 1.0) / 6.0,
        s**3 / 6.0,
    )


def spline_table(step, column, spacing, scale):
    out = jnp.zeros(step.shape, jnp.float32)
    for s in range(spacing):
        for k, weight in enumerate(spline(s, spacing)):
            if weight != 0.0:
                out = jnp.where((step == s) & (column == k), jnp.float32(weight * scale), out)
    return out


def pick(values, upper, odd):
    first = jnp.where(upper, values[2], values[0])
    second = jnp.where(upper, values[3], values[1])
    third = jnp.where(upper, values[4], values[2])
    return jnp.where(odd, second, first), jnp.where(odd, third, second)


def split(value):
    high = value.astype(jnp.bfloat16)
    low = (value - high.astype(jnp.float32)).astype(jnp.bfloat16)
    return jnp.concatenate([high, low], axis=1)


def kernel(
    sizes, subj_ref, off_ref, tmpl_ref, ctrl_ref, tout_ref, cout_ref,
    side_ref, face_ref, ext_ref, corner_ref, xw_ref, grad_ref, part_ref, below_ref, above_ref,
    rows_ref, peak_ref, warp_ref,
    side_send, side_recv, face_send, face_recv, part_send, part_recv, edge_send, edge_recv,
    rows_send, rows_recv, last_send, last_recv, peak_send, peak_recv, warp_send, warp_recv,
):
    n_z, n_y, n_s = sizes
    depth, height, width = subj_ref.shape[1:]
    halves = width // LANES
    cells = depth // KNOT
    band = cells + 3
    grid_y, grid_x = ctrl_ref.shape[3:]
    slab = lax.axis_index("slab")
    yslab = lax.axis_index("yslab")
    subj = lax.axis_index("subj")
    first_row = slab * cells

    barrier = pltpu.get_barrier_semaphore()
    for i in range(n_z):
        for k in range(n_y):
            if i or k:
                pl.semaphore_signal(
                    barrier, inc=1, device_id_type=MESH,
                    device_id={"slab": lax.rem(slab + i, n_z), "yslab": lax.rem(yslab + k, n_y)},
                )
    for i in range(1, n_s):
        pl.semaphore_signal(
            barrier, inc=1, device_id={"subj": lax.rem(subj + i, n_s)}, device_id_type=MESH
        )

    def iota(shape, axis):
        return lax.broadcasted_iota(jnp.int32, shape, axis)

    scale_x = 6.0 * KNOT_X**3

    def x_table(shape, x_axis):
        x, g = iota(shape, x_axis), iota(shape, 1 - x_axis)
        column = g - x // KNOT_X
        column = jnp.where(column < 0, column + grid_x, column)
        return spline_table(x % KNOT_X, column, KNOT_X, scale_x).astype(jnp.bfloat16)

    spread_x = x_table((grid_x, width), 1)
    spread_x = jnp.concatenate([spread_x, spread_x], axis=0)
    gather_x = x_table((width, grid_x), 0)
    gather_x = jnp.concatenate([gather_x, gather_x], axis=0)

    def y_weights(y, b):
        column = b - (yslab * height + y) // KNOT
        return spline_table(y % KNOT, column, KNOT, 1.0 / scale_x)

    rows8 = iota((SUB, LANES), 0)
    spread_y = [y_weights(rows8, (rows8 - d) % SUB) for d in range(SUB)]
    gather_y = [y_weights((rows8 - d) % SUB, rows8) for d in range(SUB)]

    def turn(value, weights):
        total = value * weights[0][None]
        for d in range(1, SUB):
            total = total + pltpu.roll(value, d, 1) * weights[d][None]
        return total

    def forward(tiles):
        mixed = turn(tiles, spread_y).reshape(band * 3 * SUB, LANES)
        out = jnp.dot(split(mixed), spread_x, preferred_element_type=jnp.float32)
        return out.reshape(band * 3, SUB, width)

    def adjoint(tiles):
        out = jnp.dot(
            split(tiles.reshape(band * 3 * SUB, width)), gather_x, preferred_element_type=jnp.float32
        )
        return turn(out.reshape(band * 3, SUB, LANES), gather_y)

    @pl.when(slab == 0)
    def _():
        below_ref[...] = jnp.zeros_like(below_ref)

    @pl.when(slab == n_z - 1)
    def _():
        above_ref[...] = jnp.zeros_like(above_ref)

    pl.semaphore_wait(barrier, n_z * n_y - 1 + n_s - 1)

    def inside(dz, dy):
        z, y = slab + dz, yslab + dy
        return (z >= 0) & (z < n_z) & (y >= 0) & (y < n_y)

    moves = []
    for dy in (-1, 1):
        moves.append((0, dy, pltpu.make_async_remote_copy(
            src_ref=subj_ref.at[0], dst_ref=side_ref.at[(1 - dy) // 2],
            send_sem=side_send.at[(1 - dy) // 2], recv_sem=side_recv.at[(1 - dy) // 2],
            device_id={"yslab": yslab + dy}, device_id_type=MESH)))
    for dz in (-1, 1):
        start = 0 if dz < 0 else depth - HALO
        for dy in (-1, 0, 1):
            a, b = (1 - dz) // 2, 1 - dy
            moves.append((dz, dy, pltpu.make_async_remote_copy(
                src_ref=subj_ref.at[0, pl.ds(start, HALO)], dst_ref=face_ref.at[a, b],
                send_sem=face_send.at[a, b], recv_sem=face_recv.at[a, b],
                device_id={"slab": slab + dz, "yslab": yslab + dy}, device_id_type=MESH)))
    for dz, dy, copy in moves:
        pl.when(inside(dz, dy))(copy.start)

    pad = jnp.zeros((SUB - grid_y, LANES), jnp.float32)
    tiles = jnp.stack([
        jnp.concatenate([ctrl_ref[0, c, first_row + a], pad], axis=0)
        for a in range(band) for c in range(3)
    ])
    xw_ref[...] = forward(tiles)

    lane = iota((1, SUB, LANES), 2)

    def place(z, tile, block):
        planes = block.shape[0]
        parts = [block[:, :, h * LANES:(h + 1) * LANES] for h in range(halves)]
        zero = jnp.zeros_like(parts[0])
        for dx in range(-HALO, HALO + 1):
            if dx == 0:
                moved = parts
            else:
                rolled = [pltpu.roll(p, (-dx) % LANES, 2) for p in parts]
                moved = []
                for h in range(halves):
                    other = h + (1 if dx > 0 else -1)
                    fill = rolled[other] if 0 <= other < halves else zero
                    edge = lane >= LANES - dx if dx > 0 else lane < -dx
                    moved.append(jnp.where(edge, fill, rolled[h]))
            for h in range(halves):
                ext_ref[dx + HALO, h, pl.ds(z, planes), tile * SUB:(tile + 1) * SUB, :] = moved[h]

    own = 4

    def place_many(tile, load):
        def body(i, carry):
            place(HALO + i * own, tile, load(pl.ds(i * own, own)).astype(jnp.float32))
            return carry
        lax.fori_loop(0, depth // own, body, 0)

    place_many(1, lambda part: subj_ref[0, part])

    for dz, dy, copy in moves:
        pl.when(inside(-dz, -dy))(copy.wait_recv)
    for d, dy in enumerate((-1, 1)):
        tile = 1 + dy

        @pl.when(inside(0, dy))
        def _():
            place_many(tile, lambda part: side_ref[d, part])

        @pl.when(jnp.logical_not(inside(0, dy)))
        def _():
            ext_ref[:, :, :, tile * SUB:(tile + 1) * SUB, :] = jnp.zeros(
                (SPAN, halves, depth + 2 * HALO, SUB, LANES), jnp.float32)
    for a, dz in enumerate((-1, 1)):
        z = 0 if dz < 0 else depth + HALO
        for b, dy in enumerate((-1, 0, 1)):
            @pl.when(inside(dz, dy))
            def _():
                place(z, b, face_ref[a, b].astype(jnp.float32))

            @pl.when(jnp.logical_not(inside(dz, dy)))
            def _():
                ext_ref[:, :, z:z + HALO, b * SUB:(b + 1) * SUB, :] = jnp.zeros(
                    (SPAN, halves, HALO, SUB, LANES), jnp.float32)

    def corners(z, carry):
        for h in range(halves):
            cut = slice(h * LANES, (h + 1) * LANES)
            bits = [(off_ref[0, i, z, :, cut] >= 0, (off_ref[0, i, z, :, cut] & 1) == 1) for i in range(3)]
            by_z = []
            for dz in range(SPAN):
                by_y = []
                for dy in range(SPAN):
                    start = SUB - HALO + dy
                    row = [ext_ref[dx, h, z + dz, start:start + SUB, :] for dx in range(SPAN)]
                    by_y.append(pick(row, *bits[2]))
                by_z.append([pick([v[x] for v in by_y], *bits[1]) for x in range(2)])
            for x in range(2):
                for y in range(2):
                    low, high = pick([v[x][y] for v in by_z], *bits[0])
                    corner_ref[0 + 2 * y + x, z, :, cut] = low
                    corner_ref[4 + 2 * y + x, z, :, cut] = high
        return carry

    lax.fori_loop(0, depth, corners, 0)

    weights_z = [spline(s, KNOT) for s in range(KNOT)]
    sends = [(inside(dz, dy), copy) for dz, dy, copy in moves]
    late = []
    warp_copies = []

    for it in range(ITERS):
        grad_ref[...] = jnp.zeros_like(grad_ref)
        if it > 0:
            for copy in warp_copies[-1]:
                copy.wait_recv()

        def cell(j, carry):
            for h in range(halves):
                cut = slice(h * LANES, (h + 1) * LANES)
                knots = [[xw_ref[(j + k) * 3 + c, :, cut] for k in range(4)] for c in range(3)]
                sums = [[None] * 4 for _ in range(3)]
                for s in range(KNOT):
                    z = j * KNOT + s
                    used = [k for k in range(4) if weights_z[s][k] != 0.0]
                    th, f = [], []
                    for c in range(3):
                        u = sum(knots[c][k] * weights_z[s][k] for k in used)
                        th.append(jnp.tanh(u))
                        f.append(0.5 + 0.5 * th[c])
                    v = [corner_ref[i, z, :, cut] for i in range(8)]
                    dx = [v[2 * i + 1] - v[2 * i] for i in range(4)]
                    ax = [v[2 * i] + dx[i] * f[2] for i in range(4)]
                    dy = [ax[1] - ax[0], ax[3] - ax[2]]
                    ay = [ax[0] + dy[0] * f[1], ax[2] + dy[1] * f[1]]
                    dxy = [dx[0] + (dx[1] - dx[0]) * f[1], dx[2] + (dx[3] - dx[2]) * f[1]]
                    slope_z = ay[1] - ay[0]
                    warped = ay[0] + slope_z * f[0]
                    slope_y = dy[0] + (dy[1] - dy[0]) * f[0]
                    slope_x = dxy[0] + (dxy[1] - dxy[0]) * f[0]
                    warp_ref[it, subj, z, :, cut] = warped
                    if it == 0:
                        current = tmpl_ref[z, :, cut]
                    else:
                        current = sum(warp_ref[it - 1, i, z, :, cut] for i in range(n_s)) * (1.0 / n_s)
                    resid = warped - current
                    for c, slope in enumerate((slope_z, slope_y, slope_x)):
                        g = resid * slope * (1.0 - th[c] * th[c])
                        for k in used:
                            term = g * weights_z[s][k]
                            sums[c][k] = term if sums[c][k] is None else sums[c][k] + term
                for c in range(3):
                    for k in range(4):
                        grad_ref[(j + k) * 3 + c, :, cut] += sums[c][k]
            return carry

        lax.fori_loop(0, cells, cell, 0)

        copies = []
        for i in range(1, n_s):
            copy = pltpu.make_async_remote_copy(
                src_ref=warp_ref.at[it, subj], dst_ref=warp_ref.at[it, subj],
                send_sem=warp_send.at[it, i], recv_sem=warp_recv.at[it, i],
                device_id={"subj": lax.rem(subj + i, n_s)}, device_id_type=MESH)
            copies.append(copy)
        warp_copies.append(copies)

        part = adjoint(grad_ref[...])
        part_ref[it, yslab] = part.reshape(band, 3, SUB, LANES).astype(jnp.bfloat16)

        part_copies = []
        for i in range(1, n_y):
            copy = pltpu.make_async_remote_copy(
                src_ref=part_ref.at[it, yslab], dst_ref=part_ref.at[it, yslab],
                send_sem=part_send.at[it, i], recv_sem=part_recv.at[it, i],
                device_id={"yslab": lax.rem(yslab + i, n_y)}, device_id_type=MESH)
            part_copies.append(copy)
        edge_copies = []
        for e, dz in enumerate((1, -1)):
            landing = below_ref if dz > 0 else above_ref
            start = cells if dz > 0 else 0
            for i in range(n_y):
                copy = pltpu.make_async_remote_copy(
                    src_ref=part_ref.at[it, yslab, pl.ds(start, 3)], dst_ref=landing.at[it, yslab],
                    send_sem=edge_send.at[it, e, i], recv_sem=edge_recv.at[it, e, i],
                    device_id={"slab": slab + dz, "yslab": lax.rem(yslab + i, n_y)},
                    device_id_type=MESH)
                edge_copies.append((inside(dz, 0), inside(-dz, 0), copy))
        for go, _, copy in edge_copies:
            pl.when(go)(copy.start)
        for copy in part_copies:
            copy.start()
        for copy in copies:
            copy.start()
        for copy in part_copies:
            copy.wait_recv()
        for _, come, copy in edge_copies:
            pl.when(come)(copy.wait_recv)
        sends += [(go, copy) for go, _, copy in edge_copies]
        sends += [(None, copy) for copy in part_copies + copies]

        def over_y(ref, where):
            return sum(ref[it, k, where].astype(jnp.float32) for k in range(n_y))

        rows = []
        for a in range(band):
            row = over_y(part_ref, a)
            if a < 3:
                row = row + over_y(below_ref, a)
            if a >= cells:
                row = row + over_y(above_ref, a - cells)
            rows.append(row)
        square = None
        for row in rows:
            here = row[0] * row[0] + row[1] * row[1] + row[2] * row[2]
            square = here if square is None else jnp.maximum(square, here)
        peak_ref[it, slab] = square
        peak_copies = []
        for i in range(1, n_z):
            copy = pltpu.make_async_remote_copy(
                src_ref=peak_ref.at[it, slab], dst_ref=peak_ref.at[it, slab],
                send_sem=peak_send.at[it, i], recv_sem=peak_recv.at[it, i],
                device_id={"slab": lax.rem(slab + i, n_z)}, device_id_type=MESH)
            peak_copies.append(copy)
        for a in range(cells):
            rows_ref[it, first_row + a] = rows[a].astype(jnp.bfloat16)

        @pl.when(slab == n_z - 1)
        def _():
            for a in range(cells, band):
                rows_ref[it, first_row + a] = rows[a].astype(jnp.bfloat16)

        for copy in peak_copies:
            copy.start()
        last = n_z * cells
        for i in range(1, n_z):
            target = {"slab": lax.rem(slab + i, n_z)}
            own_rows = rows_ref.at[it, pl.ds(first_row, cells)]
            copy = pltpu.make_async_remote_copy(
                src_ref=own_rows, dst_ref=own_rows,
                send_sem=rows_send.at[it, i], recv_sem=rows_recv.at[it, i],
                device_id=target, device_id_type=MESH)
            copy.start()
            late.append((None, copy))
            sends.append((None, copy))
            last_rows = rows_ref.at[it, pl.ds(last, 3)]
            copy = pltpu.make_async_remote_copy(
                src_ref=last_rows, dst_ref=last_rows,
                send_sem=last_send.at[it, i], recv_sem=last_recv.at[it, i],
                device_id=target, device_id_type=MESH)
            pl.when(slab == n_z - 1)(copy.start)
            late.append((lax.rem(slab - i + n_z, n_z) == n_z - 1, copy))
            sends.append((slab == n_z - 1, copy))
        sends += [(None, copy) for copy in peak_copies]

        if it + 1 < ITERS:
            change = forward(jnp.concatenate(rows, axis=0))
        for copy in peak_copies:
            copy.wait_recv()
        if it + 1 < ITERS:
            top = peak_ref[it, 0]
            for k in range(1, n_z):
                top = jnp.maximum(top, peak_ref[it, k])
            top = jnp.sqrt(jnp.max(top, axis=(0, 1), keepdims=True))
            rate = step_length / (top + tiny_term)
            xw_ref[...] = xw_ref[...] - change * rate[None]

    for copy in warp_copies[-1]:
        copy.wait_recv()
    tout_ref[...] = sum(warp_ref[ITERS - 1, i] for i in range(n_s)) * (1.0 / n_s)

    rates = []
    for it in range(ITERS):
        top = peak_ref[it, 0]
        for k in range(1, n_z):
            top = jnp.maximum(top, peak_ref[it, k])
        top = jnp.sqrt(jnp.max(top, axis=(0, 1), keepdims=True))
        rates.append(step_length / (top + tiny_term))
    for come, copy in late:
        if come is None:
            copy.wait_recv()
        else:
            pl.when(come)(copy.wait_recv)
    for a in range(cout_ref.shape[2]):
        steps = [rows_ref[it, a].astype(jnp.float32) * rates[it][None] for it in range(ITERS)]
        for c in range(3):
            value = ctrl_ref[0, c, a]
            for it in range(ITERS):
                value = value - steps[it][c, :grid_y]
            cout_ref[0, c, a] = value
    for go, copy in sends:
        if go is None:
            copy.wait_send()
        else:
            pl.when(go)(copy.wait_send)


def shards(sizes, subjects, offsets, template, control):
    n_z, n_y, n_s = sizes
    depth, height, width = subjects.shape[1:]
    halves = width // LANES
    cells = depth // KNOT
    band = cells + 3
    grid_z = control.shape[2]
    low, full = jnp.bfloat16, jnp.float32
    dma = pltpu.SemaphoreType.DMA
    scratch = [
        pltpu.VMEM((2, depth, height, width), low),
        pltpu.VMEM((2, 3, HALO, height, width), low),
        pltpu.VMEM((SPAN, halves, depth + 2 * HALO, 3 * SUB, LANES), full),
        pltpu.VMEM((8, depth, height, width), full),
        pltpu.VMEM((band * 3, SUB, width), full),
        pltpu.VMEM((band * 3, SUB, width), full),
        pltpu.VMEM((ITERS, n_y, band, 3, SUB, LANES), low),
        pltpu.VMEM((ITERS, n_y, 3, 3, SUB, LANES), low),
        pltpu.VMEM((ITERS, n_y, 3, 3, SUB, LANES), low),
        pltpu.VMEM((ITERS, grid_z, 3, SUB, LANES), low),
        pltpu.VMEM((ITERS, n_z, SUB, LANES), full),
        pltpu.VMEM((ITERS, n_s, depth, height, width), full),
        dma((2,)), dma((2,)), dma((2, 3)), dma((2, 3)),
        dma((ITERS, n_y)), dma((ITERS, n_y)), dma((ITERS, 2, n_y)), dma((ITERS, 2, n_y)),
        dma((ITERS, n_z)), dma((ITERS, n_z)), dma((ITERS, n_z)), dma((ITERS, n_z)),
        dma((ITERS, n_z)), dma((ITERS, n_z)), dma((ITERS, n_s)), dma((ITERS, n_s)),
    ]
    return pl.pallas_call(
        functools.partial(kernel, sizes),
        out_shape=(
            jax.ShapeDtypeStruct(template.shape, full),
            jax.ShapeDtypeStruct(control.shape, full),
        ),
        in_specs=[pl.BlockSpec(memory_space=pltpu.VMEM)] * 4,
        out_specs=(pl.BlockSpec(memory_space=pltpu.VMEM),) * 2,
        scratch_shapes=scratch,
        compiler_params=pltpu.CompilerParams(collective_id=0, has_side_effects=True),
        name="register",
    )(subjects, offsets, template, control)


def solution(mesh):
    in_specs = (
        P(("group", "subj"), "slab", "yslab", None),
        P(("group", "subj"), None, "slab", "yslab", None),
        P(("group", "slab"), "yslab", None),
        P(("group", "subj"), None, None, None, None),
    )
    out_specs = (P(("group", "slab"), "yslab", None), P(("group", "subj"), None, None, None, None))
    sizes = (mesh.shape["slab"], mesh.shape["yslab"], mesh.shape["subj"])
    body = functools.partial(shards, sizes)
    return jax.shard_map(body, mesh=mesh, in_specs=in_specs, out_specs=out_specs, check_vma=False)
```

time: 161 us -> 33.6 us (0.21)
  blocking collectives: 69.6 us -> 0 us
  Pallas kernels: 0 us -> 28.6 us
  waiting for transfers between devices: 20.7 us -> 0 us
  starting transfers between devices: 16.8 us -> 0 us
  between operations: 17.3 us -> 0.65 us
  other arithmetic: 16.6 us -> 0 us
  local copies, waits for them, and re-layouts: 11.8 us -> 4.16 us
  matrix products: 7.5 us -> 0 us
    psum x4 -> x0, blocking collectives: 42.9 us -> none  [the longest x2 35.2 us: from_root(): return lax.psum(kept, axis)]
    pallas_call x0 -> x1, Pallas kernels: none -> 28.6 us  [shards(): pl.pallas_call(functools.partial(kernel, sizes), out_shape=(jax.ShapeDtyp...]
    all_gather x2 -> x0, blocking collectives: 26.7 us -> none  [shards(): lax.all_gather(head_rows.astype(jnp.bfloat16), 'slab', axis=2, tiled=True)]
    psum x1 -> x0, waiting for transfers between devices: 20.5 us -> none  [shards(): current = lax.psum(warped, 'subj') / cohort]
    ppermute x6 -> x0, starting transfers between devices: 16.8 us -> none  [the longest x2 7.15 us: shifted(): return lax.ppermute(block, axis, route)]
    dot_general x12 -> x0, matrix products: 7.5 us -> none  [the longest x2 3.07 us: forward_field(): return jnp.einsum('czyg,xg->czyx', second, basis_x, precision=high)]
    another operation x6 -> x0, other arithmetic: 6.89 us -> none  [trilinear_local(): return (warped, jnp.stack([slope_z, slope_y, slope_x]))]
    unnamed x283 -> x4, local copies, waits for them, and re-layouts: 8.37 us -> 2.3 us
  transfers between devices with their start and end apart: 7 -> 0, of which waited for: 2 -> 0; matrix products, arithmetic and copies ran while one was open for 2% -> 0% of each run, Pallas kernels for 0% -> 0%
where the time goes in v1:
time: 33.6 us; the launch traced here: 33.5 us
  Pallas kernels  28.6 us (85%)
  local copies, waits for them, and re-layouts  4.16 us (12%)
  between operations  0.65 us (2%)
    pallas_call x1, Pallas kernels, shards(): pl.pallas_call(functools.partial(kernel, sizes), out_shape=(jax.ShapeDtyp...  28.6 us
    unnamed x4, local copies, waits for them, and re-layouts  2.3 us
    pallas_call x1, local copies, waits for them, and re-layouts, shards(): pl.pallas_call(functools.partial(kernel, sizes), out_shape=(jax.ShapeDtyp...  1.86 us

profile of v1, /device:TPU:0, one launch (start us, length us, event | category | flops | bytes accessed | tf_op | source)
XLA Modules:
  0.0 33.5 jit_solution(7335305283010051147)
XLA Ops:
  0.6 1.6 %copy.6.ctrl_ref = f32[1,3,19,7,128]{4,3,2,1,0:T(8,128)} copy(f32[1,3,19,7,128]{4,0,3,2,1:T(1,128)} %param.7) | data formatting | bytes 408576 | tf_op args[3]
  2.3 28.6 %register.1 = (f32[16,8,256]{2,1,0:T(8,128)}, f32[1,3,19,7,128]{4,3,2,1,0:T(8,128)}) custom-call(bf16[1,16,8,256]{3,2,1,0:T(8,128)(2,1)} %subj_ref.1, s32[1,3,16,8,256]{4,3,2,1,0:T(8,128)} %off_ref.1, f32[16,8,256]{2,1,0:T(8,128)} %tmpl_ref.1, f32[1,3,19,7,128]{4,3,2,1,0:T(8,128)} %copy.6.ctrl_ref), custom_call_target="tpu_custom_call" | custom-call | tf_op jit(solution)/shard_map/register/pallas_call | solution.py:460
  30.9 0.0 copy-start
  30.9 1.9 %copy.7 = f32[1,3,19,7,128]{4,0,3,2,1:T(1,128)} copy(f32[1,3,19,7,128]{4,3,2,1,0:T(8,128)} %get-tuple-element.3) | data formatting | bytes 408576 | tf_op jit(solution)/shard_map/register/pallas_call | solution.py:460
  32.8 0.0 copy-done
  32.8 0.7 %copy.9 = f32[16,8,256]{2,1,0:T(8,128)} copy(f32[16,8,256]{2,1,0:T(8,128)S(1)} %copy-done) | data formatting | bytes 262144
Async XLA Ops:
  30.9 1.9 %copy-start = (f32[16,8,256]{2,1,0:T(8,128)S(1)}, f32[16,8,256]{2,1,0:T(8,128)}, u32[]{:S(2)}) copy-start(f32[16,8,256]{2,1,0:T(8,128)} %get-tuple-element.6) | copy-start | bytes 393220

commit v2 on v1

--- a/solution.py
+++ b/solution.py
@@ -54,35 +54,56 @@
 
 
 def kernel(
-    sizes, subj_ref, off_ref, tmpl_ref, ctrl_ref, tout_ref, cout_ref,
+    sizes, subj_hbm, off_hbm, tmpl_hbm, ctrl_hbm, tout_hbm, cout_hbm,
+    subj_ref, off_ref, tmpl_ref, ctrl_ref, tout_ref, cout_ref, base_ref,
     side_ref, face_ref, ext_ref, corner_ref, xw_ref, grad_ref, part_ref, below_ref, above_ref,
     rows_ref, peak_ref, warp_ref,
     side_send, side_recv, face_send, face_recv, part_send, part_recv, edge_send, edge_recv,
     rows_send, rows_recv, last_send, last_recv, peak_send, peak_recv, warp_send, warp_recv,
+    relay_sem, load_sem, store_sem,
 ):
     n_z, n_y, n_s = sizes
     depth, height, width = subj_ref.shape[1:]
     halves = width // LANES
     cells = depth // KNOT
     band = cells + 3
-    grid_y, grid_x = ctrl_ref.shape[3:]
+    grid_z, grid_y, grid_x = ctrl_ref.shape[1], ctrl_ref.shape[2], ctrl_ref.shape[4]
     slab = lax.axis_index("slab")
     yslab = lax.axis_index("yslab")
     subj = lax.axis_index("subj")
     first_row = slab * cells
 
+    def inside(dz, dy):
+        z, y = slab + dz, yslab + dy
+        return (z >= 0) & (z < n_z) & (y >= 0) & (y < n_y)
+
     barrier = pltpu.get_barrier_semaphore()
-    for i in range(n_z):
-        for k in range(n_y):
-            if i or k:
-                pl.semaphore_signal(
-                    barrier, inc=1, device_id_type=MESH,
-                    device_id={"slab": lax.rem(slab + i, n_z), "yslab": lax.rem(yslab + k, n_y)},
-                )
+    for k in range(1, n_y):
+        pl.semaphore_signal(
+            barrier, inc=1, device_id={"yslab": lax.rem(yslab + k, n_y)}, device_id_type=MESH
+        )
     for i in range(1, n_s):
         pl.semaphore_signal(
             barrier, inc=1, device_id={"subj": lax.rem(subj + i, n_s)}, device_id_type=MESH
         )
+    greeted = n_y - 1 + n_s - 1
+    for dz in (-1, 1):
+        @pl.when(inside(dz, 0))
+        def _():
+            for k in range(n_y):
+                pl.semaphore_signal(
+                    barrier, inc=1, device_id_type=MESH,
+                    device_id={"slab": slab + dz, "yslab": lax.rem(yslab + k, n_y)},
+                )
+        greeted = greeted + jnp.where(inside(dz, 0), n_y, 0)
+
+    loads = [
+        pltpu.make_async_copy(src, dst, load_sem.at[i])
+        for i, (src, dst) in enumerate((
+            (subj_hbm, subj_ref), (ctrl_hbm, ctrl_ref), (off_hbm, off_ref), (tmpl_hbm, tmpl_ref)))
+    ]
+    for load in loads:
+        load.start()
 
     def iota(shape, axis):
         return lax.broadcasted_iota(jnp.int32, shape, axis)
@@ -133,11 +154,22 @@
     def _():
         above_ref[...] = jnp.zeros_like(above_ref)
 
-    pl.semaphore_wait(barrier, n_z * n_y - 1 + n_s - 1)
-
-    def inside(dz, dy):
-        z, y = slab + dz, yslab + dy
-        return (z >= 0) & (z < n_z) & (y >= 0) & (y < n_y)
+    loads[0].wait()
+    pl.semaphore_wait(barrier, greeted)
+
+    def relay_signal():
+        for d, dz in enumerate((-1, 1)):
+            @pl.when(inside(dz, 0))
+            def _():
+                pl.semaphore_signal(
+                    relay_sem.at[d], inc=1, device_id={"slab": slab + dz}, device_id_type=MESH
+                )
+
+    def relay_wait():
+        for d, dz in enumerate((1, -1)):
+            @pl.when(inside(dz, 0))
+            def _():
+                pl.semaphore_wait(relay_sem.at[d], 1)
 
     moves = []
     for dy in (-1, 1):
@@ -155,10 +187,13 @@
                 device_id={"slab": slab + dz, "yslab": yslab + dy}, device_id_type=MESH)))
     for dz, dy, copy in moves:
         pl.when(inside(dz, dy))(copy.start)
+    if n_z > 2:
+        relay_signal()
+    loads[1].wait()
 
     pad = jnp.zeros((SUB - grid_y, LANES), jnp.float32)
     tiles = jnp.stack([
-        jnp.concatenate([ctrl_ref[0, c, first_row + a], pad], axis=0)
+        jnp.concatenate([ctrl_ref[c, first_row + a, :, 0, :], pad], axis=0)
         for a in range(band) for c in range(3)
     ])
     xw_ref[...] = forward(tiles)
@@ -194,7 +229,8 @@
     place_many(1, lambda part: subj_ref[0, part])
 
     for dz, dy, copy in moves:
-        pl.when(inside(-dz, -dy))(copy.wait_recv)
+        if dz == 0:
+            pl.when(inside(-dz, -dy))(copy.wait_recv)
     for d, dy in enumerate((-1, 1)):
         tile = 1 + dy
 
@@ -206,18 +242,6 @@
         def _():
             ext_ref[:, :, :, tile * SUB:(tile + 1) * SUB, :] = jnp.zeros(
                 (SPAN, halves, depth + 2 * HALO, SUB, LANES), jnp.float32)
-    for a, dz in enumerate((-1, 1)):
-        z = 0 if dz < 0 else depth + HALO
-        for b, dy in enumerate((-1, 0, 1)):
-            @pl.when(inside(dz, dy))
-            def _():
-                place(z, b, face_ref[a, b].astype(jnp.float32))
-
-            @pl.when(jnp.logical_not(inside(dz, dy)))
-            def _():
-                ext_ref[:, :, z:z + HALO, b * SUB:(b + 1) * SUB, :] = jnp.zeros(
-                    (SPAN, halves, HALO, SUB, LANES), jnp.float32)
-
     def corners(z, carry):
         for h in range(halves):
             cut = slice(h * LANES, (h + 1) * LANES)
@@ -237,12 +261,34 @@
                     corner_ref[4 + 2 * y + x, z, :, cut] = high
         return carry
 
-    lax.fori_loop(0, depth, corners, 0)
+    loads[2].wait()
+    lax.fori_loop(HALO, depth - HALO, corners, 0)
+    for dz, dy, copy in moves:
+        if dz != 0:
+            pl.when(inside(-dz, -dy))(copy.wait_recv)
+    for a, dz in enumerate((-1, 1)):
+        z = 0 if dz < 0 else depth + HALO
+        for b, dy in enumerate((-1, 0, 1)):
+            @pl.when(inside(dz, dy))
+            def _():
+                place(z, b, face_ref[a, b].astype(jnp.float32))
+
+            @pl.when(jnp.logical_not(inside(dz, dy)))
+            def _():
+                ext_ref[:, :, z:z + HALO, b * SUB:(b + 1) * SUB, :] = jnp.zeros(
+                    (SPAN, halves, HALO, SUB, LANES), jnp.float32)
+    lax.fori_loop(0, HALO, corners, 0)
+    lax.fori_loop(depth - HALO, depth, corners, 0)
+    for _ in range(2, n_z - 1):
+        relay_wait()
+        relay_signal()
+    loads[3].wait()
 
     weights_z = [spline(s, KNOT) for s in range(KNOT)]
     sends = [(inside(dz, dy), copy) for dz, dy, copy in moves]
     late = []
     warp_copies = []
+    rates = []
 
     for it in range(ITERS):
         grad_ref[...] = jnp.zeros_like(grad_ref)
@@ -350,6 +396,8 @@
             here = row[0] * row[0] + row[1] * row[1] + row[2] * row[2]
             square = here if square is None else jnp.maximum(square, here)
         peak_ref[it, slab] = square
+        if it == 0 and n_z > 2:
+            relay_wait()
         peak_copies = []
         for i in range(1, n_z):
             copy = pltpu.make_async_remote_copy(
@@ -376,7 +424,7 @@
                 send_sem=rows_send.at[it, i], recv_sem=rows_recv.at[it, i],
                 device_id=target, device_id_type=MESH)
             copy.start()
-            late.append((None, copy))
+            late.append((it, None, copy))
             sends.append((None, copy))
             last_rows = rows_ref.at[it, pl.ds(last, 3)]
             copy = pltpu.make_async_remote_copy(
@@ -384,50 +432,60 @@
                 send_sem=last_send.at[it, i], recv_sem=last_recv.at[it, i],
                 device_id=target, device_id_type=MESH)
             pl.when(slab == n_z - 1)(copy.start)
-            late.append((lax.rem(slab - i + n_z, n_z) == n_z - 1, copy))
+            late.append((it, lax.rem(slab - i + n_z, n_z) == n_z - 1, copy))
             sends.append((slab == n_z - 1, copy))
         sends += [(None, copy) for copy in peak_copies]
 
         if it + 1 < ITERS:
             change = forward(jnp.concatenate(rows, axis=0))
+        else:
+            for copy in warp_copies[-1]:
+                copy.wait_recv()
+            tout_ref[...] = sum(warp_ref[it, i] for i in range(n_s)) * (1.0 / n_s)
+            store_tmpl = pltpu.make_async_copy(tout_ref, tout_hbm, store_sem.at[0])
+            store_tmpl.start()
+            for when, come, copy in late:
+                if when < it:
+                    if come is None:
+                        copy.wait_recv()
+                    else:
+                        pl.when(come)(copy.wait_recv)
+            for a in range(grid_z):
+                steps = [rows_ref[k, a].astype(jnp.float32) * rates[k][None] for k in range(it)]
+                for c in range(3):
+                    value = ctrl_ref[c, a, :, 0, :]
+                    for step in steps:
+                        value = value - step[c, :grid_y]
+                    base_ref[c, a, :grid_y] = value
         for copy in peak_copies:
             copy.wait_recv()
-        if it + 1 < ITERS:
-            top = peak_ref[it, 0]
-            for k in range(1, n_z):
-                top = jnp.maximum(top, peak_ref[it, k])
-            top = jnp.sqrt(jnp.max(top, axis=(0, 1), keepdims=True))
-            rate = step_length / (top + tiny_term)
-            xw_ref[...] = xw_ref[...] - change * rate[None]
-
-    for copy in warp_copies[-1]:
-        copy.wait_recv()
-    tout_ref[...] = sum(warp_ref[ITERS - 1, i] for i in range(n_s)) * (1.0 / n_s)
-
-    rates = []
-    for it in range(ITERS):
         top = peak_ref[it, 0]
         for k in range(1, n_z):
             top = jnp.maximum(top, peak_ref[it, k])
         top = jnp.sqrt(jnp.max(top, axis=(0, 1), keepdims=True))
         rates.append(step_length / (top + tiny_term))
-    for come, copy in late:
-        if come is None:
-            copy.wait_recv()
-        else:
-            pl.when(come)(copy.wait_recv)
-    for a in range(cout_ref.shape[2]):
-        steps = [rows_ref[it, a].astype(jnp.float32) * rates[it][None] for it in range(ITERS)]
+        if it + 1 < ITERS:
+            xw_ref[...] = xw_ref[...] - change * rates[it][None]
+
+    for when, come, copy in late:
+        if when == ITERS - 1:
+            if come is None:
+                copy.wait_recv()
+            else:
+                pl.when(come)(copy.wait_recv)
+    for a in range(grid_z):
+        step = rows_ref[ITERS - 1, a].astype(jnp.float32) * rates[ITERS - 1][None]
         for c in range(3):
-            value = ctrl_ref[0, c, a]
-            for it in range(ITERS):
-                value = value - steps[it][c, :grid_y]
-            cout_ref[0, c, a] = value
+            cout_ref[c, a, :, 0, :] = base_ref[c, a, :grid_y] - step[c, :grid_y]
+    store_ctrl = pltpu.make_async_copy(cout_ref, cout_hbm, store_sem.at[1])
+    store_ctrl.start()
     for go, copy in sends:
         if go is None:
             copy.wait_send()
         else:
             pl.when(go)(copy.wait_send)
+    store_tmpl.wait()
+    store_ctrl.wait()
 
 
 def shards(sizes, subjects, offsets, template, control):
@@ -437,9 +495,17 @@
     cells = depth // KNOT
     band = cells + 3
     grid_z = control.shape[2]
+    control = control.reshape(control.shape[1:4] + (1, control.shape[4]))
     low, full = jnp.bfloat16, jnp.float32
     dma = pltpu.SemaphoreType.DMA
     scratch = [
+        pltpu.VMEM(subjects.shape, low),
+        pltpu.VMEM(offsets.shape, offsets.dtype),
+        pltpu.VMEM(template.shape, full),
+        pltpu.VMEM(control.shape, full),
+        pltpu.VMEM(template.shape, full),
+        pltpu.VMEM(control.shape, full),
+        pltpu.VMEM((3, grid_z, SUB, LANES), full),
         pltpu.VMEM((2, depth, height, width), low),
         pltpu.VMEM((2, 3, HALO, height, width), low),
         pltpu.VMEM((SPAN, halves, depth + 2 * HALO, 3 * SUB, LANES), full),
@@ -456,19 +522,21 @@
         dma((ITERS, n_y)), dma((ITERS, n_y)), dma((ITERS, 2, n_y)), dma((ITERS, 2, n_y)),
         dma((ITERS, n_z)), dma((ITERS, n_z)), dma((ITERS, n_z)), dma((ITERS, n_z)),
         dma((ITERS, n_z)), dma((ITERS, n_z)), dma((ITERS, n_s)), dma((ITERS, n_s)),
+        pltpu.SemaphoreType.REGULAR((2,)), dma((4,)), dma((2,)),
     ]
-    return pl.pallas_call(
+    tmpl, ctrl = pl.pallas_call(
         functools.partial(kernel, sizes),
         out_shape=(
             jax.ShapeDtypeStruct(template.shape, full),
             jax.ShapeDtypeStruct(control.shape, full),
         ),
-        in_specs=[pl.BlockSpec(memory_space=pltpu.VMEM)] * 4,
-        out_specs=(pl.BlockSpec(memory_space=pltpu.VMEM),) * 2,
+        in_specs=[pl.BlockSpec(memory_space=pl.ANY)] * 4,
+        out_specs=(pl.BlockSpec(memory_space=pl.ANY),) * 2,
         scratch_shapes=scratch,
         compiler_params=pltpu.CompilerParams(collective_id=0, has_side_effects=True),
         name="register",
     )(subjects, offsets, template, control)
+    return tmpl, ctrl.reshape((1,) + ctrl.shape[:3] + (ctrl.shape[4],))
 
 
 def solution(mesh):

time: 33.6 us -> 28.5 us (0.85)
  Pallas kernels: 28.6 us -> 25.4 us
  local copies, waits for them, and re-layouts: 4.16 us -> 2.29 us
    pallas_call x1, Pallas kernels: 28.6 us -> 25.4 us  [shards(): pl.pallas_call(functools.partial(kernel, sizes), out_shape=(jax.ShapeDtyp...]
    pallas_call x1 -> x0, local copies, waits for them, and re-layouts: 1.86 us -> none  [shards(): pl.pallas_call(functools.partial(kernel, sizes), out_shape=(jax.ShapeDtyp...]
where the time goes in v2:
time: 28.5 us; the launch traced here: 28.4 us
  Pallas kernels  25.4 us (89%)
  local copies, waits for them, and re-layouts  2.29 us (8%)
  between operations  0.65 us (2%)
    pallas_call x1, Pallas kernels, shards(): pl.pallas_call(functools.partial(kernel, sizes), out_shape=(jax.ShapeDtyp...  25.4 us
    unnamed x4, local copies, waits for them, and re-layouts  2.29 us

profile of v2, /device:TPU:0, one launch (start us, length us, event | category | flops | bytes accessed | tf_op | source)
XLA Modules:
  0.0 28.4 jit_solution(15911419041760200213)
XLA Ops:
  0.6 25.4 %register.1 = (f32[16,8,256]{2,1,0:T(8,128)}, f32[3,19,7,1,128]{4,3,2,1,0:T(1,128)}) custom-call(bf16[1,16,8,256]{3,2,1,0:T(8,128)(2,1)} %subj_hbm.1, s32[1,3,16,8,256]{4,3,2,1,0:T(8,128)} %off_hbm.1, f32[16,8,256]{2,1,0:T(8,128)} %tmpl_hbm.1, f32[3,19,7,1,128]{4,3,2,1,0:T(1,128)} %bitcast.3), custom_call_target="tpu_custom_call" | custom-call | tf_op jit(solution)/shard_map/register/pallas_call | solution.py:527
  26.1 0.0 copy-start
  26.1 1.6 %copy.8 = f32[16,8,256]{2,1,0:T(8,128)} copy(f32[16,8,256]{2,1,0:T(8,128)} %get-tuple-element.8) | data formatting | bytes 262144
  27.7 0.0 copy-done
  27.7 0.7 %copy.9 = f32[1,3,19,7,128]{4,0,3,2,1:T(1,128)} copy(f32[1,3,19,7,128]{4,0,3,2,1:T(1,128)S(1)} %bitcast.2) | data formatting | bytes 408576
Async XLA Ops:
  26.1 1.6 %copy-start = (f32[3,19,7,1,128]{4,3,2,1,0:T(1,128)S(1)}, f32[3,19,7,1,128]{4,3,2,1,0:T(1,128)}, u32[]{:S(2)}) copy-start(f32[3,19,7,1,128]{4,3,2,1,0:T(1,128)} %get-tuple-element.5) | copy-start | bytes 612868

commit v3 on v2

--- a/solution.py
+++ b/solution.py
@@ -54,13 +54,13 @@
 
 
 def kernel(
-    sizes, subj_hbm, off_hbm, tmpl_hbm, ctrl_hbm, tout_hbm, cout_hbm,
-    subj_ref, off_ref, tmpl_ref, ctrl_ref, tout_ref, cout_ref, base_ref,
+    sizes, subj_hbm, off_hbm, tmpl_hbm, ctrl_hbm, tout_ref, cout_ref,
+    subj_ref, off_ref, tmpl_ref, ctrl_ref, base_ref,
     side_ref, face_ref, ext_ref, corner_ref, xw_ref, grad_ref, part_ref, below_ref, above_ref,
     rows_ref, peak_ref, warp_ref,
     side_send, side_recv, face_send, face_recv, part_send, part_recv, edge_send, edge_recv,
     rows_send, rows_recv, last_send, last_recv, peak_send, peak_recv, warp_send, warp_recv,
-    relay_sem, load_sem, store_sem,
+    relay_sem, load_sem,
 ):
     n_z, n_y, n_s = sizes
     depth, height, width = subj_ref.shape[1:]
@@ -395,7 +395,9 @@
         for row in rows:
             here = row[0] * row[0] + row[1] * row[1] + row[2] * row[2]
             square = here if square is None else jnp.maximum(square, here)
-        peak_ref[it, slab] = square
+        for d in (1, 2, 4):
+            square = jnp.maximum(square, pltpu.roll(square, d, 0))
+        peak_ref[it, slab] = square[:1]
         if it == 0 and n_z > 2:
             relay_wait()
         peak_copies = []
@@ -442,8 +444,6 @@
             for copy in warp_copies[-1]:
                 copy.wait_recv()
             tout_ref[...] = sum(warp_ref[it, i] for i in range(n_s)) * (1.0 / n_s)
-            store_tmpl = pltpu.make_async_copy(tout_ref, tout_hbm, store_sem.at[0])
-            store_tmpl.start()
             for when, come, copy in late:
                 if when < it:
                     if come is None:
@@ -477,15 +477,11 @@
         step = rows_ref[ITERS - 1, a].astype(jnp.float32) * rates[ITERS - 1][None]
         for c in range(3):
             cout_ref[c, a, :, 0, :] = base_ref[c, a, :grid_y] - step[c, :grid_y]
-    store_ctrl = pltpu.make_async_copy(cout_ref, cout_hbm, store_sem.at[1])
-    store_ctrl.start()
     for go, copy in sends:
         if go is None:
             copy.wait_send()
         else:
             pl.when(go)(copy.wait_send)
-    store_tmpl.wait()
-    store_ctrl.wait()
 
 
 def shards(sizes, subjects, offsets, template, control):
@@ -503,8 +499,6 @@
         pltpu.VMEM(offsets.shape, offsets.dtype),
         pltpu.VMEM(template.shape, full),
         pltpu.VMEM(control.shape, full),
-        pltpu.VMEM(template.shape, full),
-        pltpu.VMEM(control.shape, full),
         pltpu.VMEM((3, grid_z, SUB, LANES), full),
         pltpu.VMEM((2, depth, height, width), low),
         pltpu.VMEM((2, 3, HALO, height, width), low),
@@ -516,22 +510,22 @@
         pltpu.VMEM((ITERS, n_y, 3, 3, SUB, LANES), low),
         pltpu.VMEM((ITERS, n_y, 3, 3, SUB, LANES), low),
         pltpu.VMEM((ITERS, grid_z, 3, SUB, LANES), low),
-        pltpu.VMEM((ITERS, n_z, SUB, LANES), full),
+        pltpu.VMEM((ITERS, n_z, 1, LANES), full),
         pltpu.VMEM((ITERS, n_s, depth, height, width), full),
         dma((2,)), dma((2,)), dma((2, 3)), dma((2, 3)),
         dma((ITERS, n_y)), dma((ITERS, n_y)), dma((ITERS, 2, n_y)), dma((ITERS, 2, n_y)),
         dma((ITERS, n_z)), dma((ITERS, n_z)), dma((ITERS, n_z)), dma((ITERS, n_z)),
         dma((ITERS, n_z)), dma((ITERS, n_z)), dma((ITERS, n_s)), dma((ITERS, n_s)),
-        pltpu.SemaphoreType.REGULAR((2,)), dma((4,)), dma((2,)),
+        pltpu.SemaphoreType.REGULAR((2,)), dma((4,)),
     ]
     tmpl, ctrl = pl.pallas_call(
         functools.partial(kernel, sizes),
         out_shape=(
-            jax.ShapeDtypeStruct(template.shape, full),
-            jax.ShapeDtypeStruct(control.shape, full),
+            pltpu.VMEM(template.shape, full),
+            pltpu.VMEM(control.shape, full),
         ),
         in_specs=[pl.BlockSpec(memory_space=pl.ANY)] * 4,
-        out_specs=(pl.BlockSpec(memory_space=pl.ANY),) * 2,
+        out_specs=(pl.BlockSpec(memory_space=pltpu.VMEM),) * 2,
         scratch_shapes=scratch,
         compiler_params=pltpu.CompilerParams(collective_id=0, has_side_effects=True),
         name="register",

time: 28.5 us -> 26.4 us (0.926)
  Pallas kernels: 25.4 us -> 24.2 us
  local copies, waits for them, and re-layouts: 2.29 us -> 1.34 us
    pallas_call x1, Pallas kernels: 25.4 us -> 24.2 us  [shards(): pl.pallas_call(functools.partial(kernel, sizes), out_shape=(pltpu.VMEM(te...]
    unnamed x4 -> x2, local copies, waits for them, and re-layouts: 2.29 us -> 1.34 us
where the time goes in v3:
time: 26.4 us; the launch traced here: 26.2 us
  Pallas kernels  24.2 us (92%)
  local copies, waits for them, and re-layouts  1.34 us (5%)
  between operations  0.64 us (2%)
    pallas_call x1, Pallas kernels, shards(): pl.pallas_call(functools.partial(kernel, sizes), out_shape=(pltpu.VMEM(te...  24.2 us
    unnamed x2, local copies, waits for them, and re-layouts  1.34 us

profile of v3, /device:TPU:0, one launch (start us, length us, event | category | flops | bytes accessed | tf_op | source)
XLA Modules:
  0.0 26.2 jit_solution(10297319091437569223)
XLA Ops:
  0.6 24.2 %register.1 = (f32[16,8,256]{2,1,0:T(8,128)S(1)}, f32[3,19,7,1,128]{4,3,2,1,0:T(1,128)S(1)}) custom-call(bf16[1,16,8,256]{3,2,1,0:T(8,128)(2,1)} %subj_hbm.1, s32[1,3,16,8,256]{4,3,2,1,0:T(8,128)} %off_hbm.1, f32[16,8,256]{2,1,0:T(8,128)} %tmpl_hbm.1, f32[3,19,7,1,128]{4,3,2,1,0:T(1,128)} %bitcast.3), custom_call_target="tpu_custom_call" | custom-call | tf_op jit(solution)/shard_map/register/pallas_call | solution.py:521
  24.9 0.7 %copy.8 = f32[16,8,256]{2,1,0:T(8,128)} copy(f32[16,8,256]{2,1,0:T(8,128)S(1)} %get-tuple-element.6) | data formatting | bytes 262144
  25.5 0.7 %copy.9 = f32[1,3,19,7,128]{4,0,3,2,1:T(1,128)} copy(f32[1,3,19,7,128]{4,0,3,2,1:T(1,128)S(1)} %bitcast.2) | data formatting | bytes 408576
